TPU v7x, 128 devices: a whole 4x4x4 slice. The times are simulated.
128 devices in a mesh: phase: 4 (over z_hi, core), blk: 32 (over y, z_lo, x).
Axes of the slice: x: 4, y: 4, z: 4 (z_hi: 2, z_lo: 2; z = z_hi * 2 + z_lo), core: 2. Of those that a mesh axis runs over, the one named last changes fastest.
Arguments:
- tokens: bfloat16 [2, 256, 6144], P(None, 'blk'), may hold values from -6 to 6
- norm_gain: float32 [4, 6144], P('phase'), may hold values from 0.5 to 1.5
- up_weight: bfloat16 [4, 6144, 24576], P('phase', None, 'blk'), may hold values from -0.078125 to 0.078125
- up_bias: float32 [4, 24576], P('phase', 'blk'), may hold values from -3 to 3
- down_weight: bfloat16 [4, 24576, 6144], P('phase', 'blk'), may hold values from -0.0390625 to 0.0390625
- down_bias: float32 [4, 6144], P('phase'), may hold values from -3 to 3
Outputs:
- sections: bfloat16 [4, 2, 256, 6144], P('phase', None, 'blk')
All inputs are finite; a program needn't handle non-finite values.
Results may differ from a plain program's by a relative error of at most 0.022.
Values may be sent and summed in bfloat16 or wider, within the bound.
A program may use at most 128 MiB of HBM per device.

v0:
```python
import jax
import jax.numpy as jnp
from jax import lax
from jax.sharding import PartitionSpec as P


def from_behind(block, axis, distance):
    devices = range(lax.axis_size(axis))
    route = [(i - distance, i) for i in devices if i - distance in devices]
    return lax.ppermute(block, axis, route)


def on_device(tokens, norm_gain, up_weight, up_bias, down_weight, down_bias):
    gain_row = norm_gain[0]
    w_up = up_weight[0]
    b_up = up_bias[0]
    w_down = down_weight[0]
    b_down = down_bias[0]
    num_micro, num_rows, feature_dim = tokens.shape
    phase_index = lax.axis_index("phase")
    num_phases = lax.axis_size("phase")
    results = [jnp.zeros((num_rows, feature_dim), jnp.bfloat16) for index in range(num_micro)]
    previous = results[0]
    for moment in range(num_micro + num_phases - 1):
        entering = tokens[min(moment, num_micro - 1)]
        if moment == 0:
            incoming = jnp.zeros_like(entering)
        else:
            incoming = from_behind(previous, "phase", 1)
        inputs = jnp.where(phase_index == 0, entering, incoming)
        widened = inputs.astype(jnp.float32)
        row_mean = jnp.mean(widened, axis=-1, keepdims=True)
        centered = widened - row_mean
        row_var = jnp.mean(centered * centered, axis=-1, keepdims=True)
        normed = (centered * lax.rsqrt(row_var + 1e-05) * gain_row).astype(jnp.bfloat16)
        hidden = jax.nn.gelu(
            jnp.dot(
                lax.all_gather(normed, "blk", axis=0, tiled=True),
                w_up,
                preferred_element_type=jnp.float32,
            )
            + b_up
        ).astype(jnp.bfloat16)
        branch = lax.psum_scatter(
            jnp.dot(hidden, w_down, preferred_element_type=jnp.float32).astype(jnp.bfloat16),
            "blk",
            scatter_dimension=0,
            tiled=True,
        ).astype(jnp.float32)
        current = (widened + branch + b_down).astype(jnp.bfloat16)
        for index in range(num_micro):
            results[index] = jnp.where(moment - phase_index == index, current, results[index])
        previous = current
    return jnp.stack(results)[None]


def solution(mesh):
    return jax.shard_map(
        on_device,
        mesh=mesh,
        in_specs=(
            P(None, "blk", None),
            P("phase", None),
            P("phase", None, "blk"),
            P("phase", "blk"),
            P("phase", "blk", None),
            P("phase", None),
        ),
        out_specs=P("phase", None, "blk", None),
        check_vma=False,
    )
```

profile of v0, /device:TPU:65, one launch (start us, length us, event | category | flops | bytes accessed | tf_op | source)
XLA Modules:
  0.0 1707.3 jit_solution(6836744143006420391)
XLA Ops:
  8.7 1.7 fusion.171
  11.2 134.1 %all-gather.6.cloned.1.call-done = bf16[256,6144]{1,0:T(8,128)(2,1)} async-done(((bf16[8,6144]{1,0:T(8,128)(2,1)}), bf16[256,6144]{1,0:T(8,128)(2,1)}) %all-gather.6.cloned.1.call-update) | async-done | bytes 3145744 | tf_op jit(solution)/shard_map/all_gather | solution.py:38
  145.3 15.7 fusion.20
  161.1 164.7 %reduce-scatter.6.cloned.1.call-done = bf16[8,6144]{1,0:T(8,128)(2,1)} async-done(((bf16[256,6144]{1,0:T(8,128)(2,1)}), bf16[8,6144]{1,0:T(8,128)(2,1)}) %reduce-scatter.6.cloned.1.call-update) | async-done | bytes 98320 | tf_op jit(solution)/shard_map/reduce_scatter | solution.py:44
  326.7 1.3 collective-permute-start
  328.0 25.7 %collective-permute-done = bf16[8,6144]{1,0:T(8,128)(2,1)S(1)} collective-permute-done((bf16[8,6144]{1,0:T(8,128)(2,1)S(1)}, bf16[8,6144]{1,0:T(8,128)(2,1)S(1)}, u32[]{:S(2)}, u32[]{:S(2)}) %collective-permute-start) | collective-permute-done | bytes 98336 | tf_op jit(solution)/shard_map/ppermute | solution.py:10
  354.9 133.6 %all-gather.8.cloned.1.call-done = bf16[256,6144]{1,0:T(8,128)(2,1)} async-done(((bf16[8,6144]{1,0:T(8,128)(2,1)}), bf16[256,6144]{1,0:T(8,128)(2,1)}) %all-gather.8.cloned.1.call-update) | async-done | bytes 3145744 | tf_op jit(solution)/shard_map/all_gather | solution.py:38
  488.5 15.7 fusion.23
  504.3 164.5 %reduce-scatter.8.cloned.1.call-done = bf16[8,6144]{1,0:T(8,128)(2,1)} async-done(((bf16[256,6144]{1,0:T(8,128)(2,1)}), bf16[8,6144]{1,0:T(8,128)(2,1)}) %reduce-scatter.8.cloned.1.call-update) | async-done | bytes 98320 | tf_op jit(solution)/shard_map/reduce_scatter | solution.py:44
  669.8 1.3 collective-permute-start.1
  671.1 26.1 %collective-permute-done.1 = bf16[8,6144]{1,0:T(8,128)(2,1)S(1)} collective-permute-done((bf16[8,6144]{1,0:T(8,128)(2,1)S(1)}, bf16[8,6144]{1,0:T(8,128)(2,1)S(1)}, u32[]{:S(2)}, u32[]{:S(2)}) %collective-permute-start.1) | collective-permute-done | bytes 98336 | tf_op jit(solution)/shard_map/ppermute | solution.py:10
  698.6 133.0 %all-gather.10.cloned.1.call-done = bf16[256,6144]{1,0:T(8,128)(2,1)} async-done(((bf16[8,6144]{1,0:T(8,128)(2,1)}), bf16[256,6144]{1,0:T(8,128)(2,1)}) %all-gather.10.cloned.1.call-update) | async-done | bytes 3145744 | tf_op jit(solution)/shard_map/all_gather | solution.py:38
  831.6 15.7 fusion.26
  847.4 164.3 %reduce-scatter.10.cloned.1.call-done = bf16[8,6144]{1,0:T(8,128)(2,1)} async-done(((bf16[256,6144]{1,0:T(8,128)(2,1)}), bf16[8,6144]{1,0:T(8,128)(2,1)}) %reduce-scatter.10.cloned.1.call-update) | async-done | bytes 98320 | tf_op jit(solution)/shard_map/reduce_scatter | solution.py:44
  1012.7 1.3 collective-permute-start.2
  1014.0 26.7 %collective-permute-done.2 = bf16[8,6144]{1,0:T(8,128)(2,1)S(1)} collective-permute-done((bf16[8,6144]{1,0:T(8,128)(2,1)S(1)}, bf16[8,6144]{1,0:T(8,128)(2,1)S(1)}, u32[]{:S(2)}, u32[]{:S(2)}) %collective-permute-start.2) | collective-permute-done | bytes 98336 | tf_op jit(solution)/shard_map/ppermute | solution.py:10
  1041.9 133.6 %all-gather.12.cloned.1.call-done = bf16[256,6144]{1,0:T(8,128)(2,1)} async-done(((bf16[8,6144]{1,0:T(8,128)(2,1)}), bf16[256,6144]{1,0:T(8,128)(2,1)}) %all-gather.12.cloned.1.call-update) | async-done | bytes 3145744 | tf_op jit(solution)/shard_map/all_gather | solution.py:38
  1175.6 15.7 fusion.29
  1191.4 164.2 %reduce-scatter.12.cloned.1.call-done = bf16[8,6144]{1,0:T(8,128)(2,1)} async-done(((bf16[256,6144]{1,0:T(8,128)(2,1)}), bf16[8,6144]{1,0:T(8,128)(2,1)}) %reduce-scatter.12.cloned.1.call-update) | async-done | bytes 98320 | tf_op jit(solution)/shard_map/reduce_scatter | solution.py:44
  1356.5 1.3 collective-permute-start.3
  1357.8 26.4 %collective-permute-done.3 = bf16[8,6144]{1,0:T(8,128)(2,1)S(1)} collective-permute-done((bf16[8,6144]{1,0:T(8,128)(2,1)S(1)}, bf16[8,6144]{1,0:T(8,128)(2,1)S(1)}, u32[]{:S(2)}, u32[]{:S(2)}) %collective-permute-start.3) | collective-permute-done | bytes 98336 | tf_op jit(solution)/shard_map/ppermute | solution.py:10
  1385.6 133.0 %all-gather.14.cloned.1.call-done = bf16[256,6144]{1,0:T(8,128)(2,1)} async-done(((bf16[8,6144]{1,0:T(8,128)(2,1)}), bf16[256,6144]{1,0:T(8,128)(2,1)}) %all-gather.14.cloned.1.call-update) | async-done | bytes 3145744 | tf_op jit(solution)/shard_map/all_gather | solution.py:38
  1518.7 15.7 fusion.32
  1534.4 164.4 %reduce-scatter.14.cloned.1.call-done = bf16[8,6144]{1,0:T(8,128)(2,1)} async-done(((bf16[256,6144]{1,0:T(8,128)(2,1)}), bf16[8,6144]{1,0:T(8,128)(2,1)}) %reduce-scatter.14.cloned.1.call-update) | async-done | bytes 98320 | tf_op jit(solution)/shard_map/reduce_scatter | solution.py:44
  (57 shorter events, 13.9 us)
Async XLA Ops:
  6.5 138.7 %all-gather.6.cloned.1.call-start = ((), (), s32[]{:S(2)}) async-start(), calls=%async_computation.5 | async-start | bytes 3244032 | tf_op jit(solution)/shard_map/all_gather | solution.py:38
  10.4 315.3 %reduce-scatter.6.cloned.1.call-start = ((), (), s32[]{:S(2)}) async-start(), calls=%async_computation.6 | async-start | bytes 3244032 | tf_op jit(solution)/shard_map/reduce_scatter | solution.py:44
  11.2 314.6 %copy-start = (bf16[2,8,6144]{2,1,0:T(8,128)(2,1)S(1)}, bf16[2,8,6144]{2,1,0:T(8,128)(2,1)}, u32[]{:S(2)}) copy-start(bf16[2,8,6144]{2,1,0:T(8,128)(2,1)} %param.6) | copy-start | bytes 589828
  11.2 314.6 %copy-start.1 = (f32[1,6144]{1,0:T(1,128)S(1)}, f32[1,6144]{1,0:T(1,128)}, u32[]{:S(2)}) copy-start(f32[1,6144]{1,0:T(1,128)} %param.11) | copy-start | bytes 73732
  11.2 342.9 %copy-start.2 = (f32[1,6144]{1,0:T(1,128)S(1)}, f32[1,6144]{1,0:T(1,128)}, u32[]{:S(2)}) copy-start(f32[1,6144]{1,0:T(1,128)} %param.7) | copy-start | bytes 73732
  161.0 327.5 %all-gather.8.cloned.1.call-start = ((), (), s32[]{:S(2)}) async-start(), calls=%async_computation.7 | async-start | bytes 3244032 | tf_op jit(solution)/shard_map/all_gather | solution.py:38
  326.7 27.0 %collective-permute-start = (bf16[8,6144]{1,0:T(8,128)(2,1)S(1)}, bf16[8,6144]{1,0:T(8,128)(2,1)S(1)}, u32[]{:S(2)}, u32[]{:S(2)}) collective-permute-start(bf16[8,6144]{1,0:T(8,128)(2,1)S(1)} %fusion.173), channel_id=1, source_target_pairs={{0,32},{32,64},{64,96},{1,33},{33,65},{65,97},{2,34},{34,66},{66,9... | collective-permute-start | bytes 294920 | tf_op jit(solution)/shard_map/ppermute | solution.py:10
  354.9 314.0 %reduce-scatter.8.cloned.1.call-start = ((), (), s32[]{:S(2)}) async-start(), calls=%async_computation.8 | async-start | bytes 3244032 | tf_op jit(solution)/shard_map/reduce_scatter | solution.py:44
  504.3 327.3 %all-gather.10.cloned.1.call-start = ((), (), s32[]{:S(2)}) async-start(), calls=%async_computation.9 | async-start | bytes 3244032 | tf_op jit(solution)/shard_map/all_gather | solution.py:38
  669.8 27.4 %collective-permute-start.1 = (bf16[8,6144]{1,0:T(8,128)(2,1)S(1)}, bf16[8,6144]{1,0:T(8,128)(2,1)S(1)}, u32[]{:S(2)}, u32[]{:S(2)}) collective-permute-start(bf16[8,6144]{1,0:T(8,128)(2,1)S(1)} %fusion.175), channel_id=1, source_target_pairs={{0,32},{32,64},{64,96},{1,33},{33,65},{65,97},{2,34},{34,66},{66,9... | collective-permute-start | bytes 294920 | tf_op jit(solution)/shard_map/ppermute | solution.py:10
  698.3 313.4 %reduce-scatter.10.cloned.1.call-start = ((), (), s32[]{:S(2)}) async-start(), calls=%async_computation.10 | async-start | bytes 3244032 | tf_op jit(solution)/shard_map/reduce_scatter | solution.py:44
  847.4 328.2 %all-gather.12.cloned.1.call-start = ((), (), s32[]{:S(2)}) async-start(), calls=%async_computation.11 | async-start | bytes 3244032 | tf_op jit(solution)/shard_map/all_gather | solution.py:38
  1012.7 28.0 %collective-permute-start.2 = (bf16[8,6144]{1,0:T(8,128)(2,1)S(1)}, bf16[8,6144]{1,0:T(8,128)(2,1)S(1)}, u32[]{:S(2)}, u32[]{:S(2)}) collective-permute-start(bf16[8,6144]{1,0:T(8,128)(2,1)S(1)} %fusion.177), channel_id=1, source_target_pairs={{0,32},{32,64},{64,96},{1,33},{33,65},{65,97},{2,34},{34,66},{66,9... | collective-permute-start | bytes 294920 | tf_op jit(solution)/shard_map/ppermute | solution.py:10
  1041.9 313.7 %reduce-scatter.12.cloned.1.call-start = ((), (), s32[]{:S(2)}) async-start(), calls=%async_computation.12 | async-start | bytes 3244032 | tf_op jit(solution)/shard_map/reduce_scatter | solution.py:44
  1191.3 327.3 %all-gather.14.cloned.1.call-start = ((), (), s32[]{:S(2)}) async-start(), calls=%async_computation.13 | async-start | bytes 3244032 | tf_op jit(solution)/shard_map/all_gather | solution.py:38
  1356.5 27.7 %collective-permute-start.3 = (bf16[8,6144]{1,0:T(8,128)(2,1)S(1)}, bf16[8,6144]{1,0:T(8,128)(2,1)S(1)}, u32[]{:S(2)}, u32[]{:S(2)}) collective-permute-start(bf16[8,6144]{1,0:T(8,128)(2,1)S(1)} %fusion.179), channel_id=1, source_target_pairs={{0,32},{32,64},{64,96},{1,33},{33,65},{65,97},{2,34},{34,66},{66,9... | collective-permute-start | bytes 294920 | tf_op jit(solution)/shard_map/ppermute | solution.py:10
  1385.4 313.4 %reduce-scatter.14.cloned.1.call-start = ((), (), s32[]{:S(2)}) async-start(), calls=%async_computation.14 | async-start | bytes 3244032 | tf_op jit(solution)/shard_map/reduce_scatter | solution.py:44
Sparse Core Ops, SparseCore 0:
  10.5 134.6 all-gather.5
  161.2 164.5 reduce-scatter.5
  355.0 133.5 all-gather.7
  504.4 164.3 reduce-scatter.7
  698.4 133.1 all-gather.9
  847.5 164.2 reduce-scatter.9
  1042.0 133.5 all-gather.11
  1191.5 164.0 reduce-scatter.11
  1385.5 133.1 all-gather.13
  1534.5 164.2 reduce-scatter.13
where the time goes:
time: 1730 us; the launch traced here: 1710 us
  waiting for transfers between devices  1590 us (92%)
  matrix products  78.7 us (5%)
    reduce_scatter x5, waiting for transfers between devices, on_device(): lax.psum_scatter(jnp.dot(hidden, w_down, preferred_element_type=jnp.float...  822 us
    all_gather x5, waiting for transfers between devices, on_device(): lax.all_gather(normed, 'blk', axis=0, tiled=True)  667 us
    ppermute x4, waiting for transfers between devices, from_behind(): return lax.ppermute(block, axis, route)  105 us
    dot_general x5, matrix products, on_device(): jnp.dot(hidden, w_down, preferred_element_type=jnp.float32)  78.7 us
  transfers between devices with their start and end apart: 14, of which 14 were waited for; matrix products, arithmetic and copies ran while one was open for 0% of the time, Pallas kernels for 0%

commit v1 on v0

v1 whole, which is shorter than its diff:
```python
import functools

import jax
import jax.numpy as jnp
from jax import lax
from jax.experimental import pallas as pl
from jax.experimental.pallas import tpu as pltpu
from jax.sharding import PartitionSpec as P

MESH = pl.DeviceIdType.MESH
SIDE = 4
F32, BF16 = jnp.float32, jnp.bfloat16


def kernel(phases, tokens, gain, b_up, b_down, w_up_hbm, w_down_hbm, out,
           w_up, w_down, x_in, gathered, hidden, partial, far1, near1, sum1, far2, near2,
           z_own, z_got, x_out,
           w_sem, zx_sem, in_sem, ag_send, ag_recv, rs_send, rs_recv, z_send, z_recv, next_send):
    micro, _, depth = tokens.shape
    quarter = depth // 4
    half = depth // 2
    units = w_up.shape[1]
    rows = 16 * SIDE * SIDE
    phase = lax.axis_index("phase")
    blk = lax.axis_index("blk")
    y, z, x = blk // 8, (blk // 4) % 2, blk % 4

    def at(yy, zz, xx):
        return (phase, ((yy % SIDE) * 2 + zz) * 4 + xx % SIDE)

    def turned(where, odd):
        return jnp.where(odd == 1, y * 8 + (1 - z) * 4 + x, where)

    step_to = {("x", 1): at(y, z, x + 1), ("x", -1): at(y, z, x + 3),
               ("y", 1): at(y + 1, z, x), ("y", -1): at(y + 3, z, x)}
    z_peer = at(y, 1 - z, x)
    after = ((phase + 1) % phases, turned(blk, phase % 2))
    before = ((phase + phases - 1) % phases, turned(blk, (phase + 1) % 2))

    up_copy = pltpu.make_async_copy(w_up_hbm.at[0], w_up, w_sem.at[0])
    down_copy = pltpu.make_async_copy(w_down_hbm.at[0], w_down, w_sem.at[1])
    up_copy.start()
    down_copy.start()

    barrier = pltpu.get_barrier_semaphore()
    friends = list(step_to.values()) + [z_peer, after, before]
    for friend in friends:
        pl.semaphore_signal(barrier, inc=1, device_id=friend, device_id_type=MESH)
    pl.semaphore_wait(barrier, len(friends))

    def zx_copy(m):
        return pltpu.make_async_remote_copy(
            src_ref=tokens.at[m], dst_ref=x_in.at[m, z], send_sem=zx_sem.at[m], recv_sem=in_sem.at[m],
            device_id=z_peer, device_id_type=MESH)

    def next_copy(m):
        return pltpu.make_async_remote_copy(
            src_ref=x_out.at[m], dst_ref=x_in.at[m], send_sem=next_send.at[m], recv_sem=in_sem.at[m],
            device_id=after, device_id_type=MESH)

    @pl.when(phase == 0)
    def _():
        for m in range(micro):
            zx_copy(m).start()
        for m in range(micro):
            x_in[m, z] = tokens[m]

    def send(src, dst, send_sem, recv_sem, device):
        copy = pltpu.make_async_remote_copy(src_ref=src, dst_ref=dst, send_sem=send_sem, recv_sem=recv_sem,
                                            device_id=device, device_id_type=MESH)
        copy.start()
        return copy

    def one(m, carry):
        @pl.when(phase == 0)
        def _():
            zx_copy(m).wait_recv()

        @pl.when(phase > 0)
        def _():
            next_copy(m).wait_recv()

        normed = []
        for row in range(2):
            wide = x_in[m, row].astype(F32)
            mean = jnp.mean(wide, axis=-1, keepdims=True)
            centered = wide - mean
            var = jnp.mean(centered * centered, axis=-1, keepdims=True)
            normed.append(centered * lax.rsqrt(var + 1e-05) * gain[...])
        gathered[m, y, x] = jnp.concatenate(normed, axis=0).astype(BF16)

        sends = []
        first_axis, second_axis = ("x", "y"), ("y", "x")
        first, second = (x, y), (y, x)

        def slot(h, s, f):
            return gathered.at[m, s % SIDE, f % SIDE] if h == 0 else gathered.at[m, f % SIDE, s % SIDE]

        def spread(h, s, f, start, size, axis, way, index):
            block = slot(h, s, f).at[:, pl.ds(start, size)]
            d = 0 if way == 1 else 1
            sends.append(send(block, block, ag_send.at[h, d, index], ag_recv.at[m, h, d, index], step_to[axis, way]))

        def arrived(h, d, index, size):
            block = gathered.at[m, 0, 0, :, pl.ds(0, size)]
            pltpu.make_async_remote_copy(src_ref=block, dst_ref=block, send_sem=ag_send.at[h, d, index],
                                         recv_sem=ag_recv.at[m, h, d, index], device_id=z_peer,
                                         device_id_type=MESH).wait_recv()

        for h in range(2):
            for way in (1, -1):
                spread(h, second[h], first[h], h * half, half, first_axis[h], way, 0)
        for h in range(2):
            for way in (1, -1):
                spread(h, second[h], first[h], h * half, half, second_axis[h], way, 2)
        for d, way in ((0, 1), (1, -1)):
            for h in range(2):
                arrived(h, d, 0, half)
                spread(h, second[h], first[h] + (SIDE - way), h * half + d * quarter, quarter, first_axis[h], way, 1)
        for d, way in ((0, 1), (1, -1)):
            for h in range(2):
                for to in (1, -1):
                    spread(h, second[h], first[h] + (SIDE - way), h * half, half, second_axis[h], to, 3 + d)
        for h in range(2):
            arrived(h, 0, 1, quarter)
            arrived(h, 1, 1, quarter)
            for to in (1, -1):
                spread(h, second[h], first[h] + 2, h * half, half, second_axis[h], to, 5)
        shift = (0, SIDE - 1, 1, 2)
        for index in range(4):
            for d, way in ((0, 1), (1, -1)):
                for h in range(2):
                    arrived(h, d, 2 + index, half)
                    spread(h, second[h] + (SIDE - way), first[h] + shift[index], h * half + d * quarter, quarter,
                           second_axis[h], way, 6 + index)
        for index in range(4):
            for d in range(2):
                for h in range(2):
                    arrived(h, d, 6 + index, quarter)

        @pl.when(m == 0)
        def _():
            up_copy.wait()

        wide_n = min(256, units)

        def up(n, c):
            columns = pl.ds(pl.multiple_of(n * wide_n, wide_n), wide_n)
            block = gathered[m].reshape(rows, depth)
            value = jnp.dot(block, w_up[:, columns], preferred_element_type=F32) + b_up[:, columns]
            hidden[:, columns] = jax.nn.gelu(value).astype(BF16)
            return c

        lax.fori_loop(0, units // wide_n, up, 0)

        @pl.when(m == 0)
        def _():
            down_copy.wait()

        wide_q = min(512, quarter)

        def strip(h, s, start, size):
            cut = pl.ds(start, size)
            return partial.at[m, s % SIDE, :, :, cut] if h == 0 else partial.at[m, :, s % SIDE, :, cut]

        def reduce1(h, src, dst, way, index):
            d = 0 if way == 1 else 1
            sends.append(send(src, dst, rs_send.at[h, 0, d, index], rs_recv.at[m, h, 0, d, index],
                              step_to[second_axis[h], way]))

        def reduce2(h, src, dst, way, index):
            d = 0 if way == 1 else 1
            sends.append(send(src, dst, rs_send.at[h, 1, d, index], rs_recv.at[m, h, 1, d, index],
                              step_to[first_axis[h], way]))

        def got(ref, h, stage, d, index):
            pltpu.make_async_remote_copy(src_ref=ref, dst_ref=ref, send_sem=rs_send.at[h, stage, d, index],
                                         recv_sem=rs_recv.at[m, h, stage, d, index], device_id=z_peer,
                                         device_id_type=MESH).wait_recv()

        for d, way in ((0, 1), (1, -1)):
            for h in range(2):
                base = h * half + d * quarter

                def down(n, c):
                    columns = pl.ds(pl.multiple_of(base + n * wide_q, wide_q), wide_q)
                    value = jnp.dot(hidden[...], w_down[:, columns], preferred_element_type=F32)
                    partial[m, :, :, :, columns] = value.astype(BF16).reshape(SIDE, SIDE, 16, wide_q)
                    return c

                lax.fori_loop(0, quarter // wide_q, down, 0)
                reduce1(h, strip(h, second[h] + 2, base, quarter), far1.at[m, h, d], way, 0)
                reduce1(h, strip(h, second[h] + way + SIDE * 0 + (SIDE - 2 * way), base, quarter),
                        near1.at[m, h, 1 - d, d], -way, 1 + d)
        for d, way in ((0, 1), (1, -1)):
            for h in range(2):
                base = h * half + d * quarter
                got(far1.at[m, h, d], h, 0, d, 0)
                target = strip(h, second[h] + SIDE + way, base, quarter)

                def fold(i, c):
                    target[i] = (target[i].astype(F32) + far1[m, h, d, i].astype(F32)).astype(BF16)
                    return c

                lax.fori_loop(0, SIDE, fold, 0)
                reduce1(h, target, near1.at[m, h, d, d], way, 1 + d)
        for h in range(2):
            for part in range(2):
                for d in range(2):
                    got(near1.at[m, h, d, part], h, 0, d, 1 + part)
                mine = strip(h, second[h], h * half + part * quarter, quarter)

                def fold(i, c):
                    total = mine[i].astype(F32) + near1[m, h, 0, part, i].astype(F32) + near1[m, h, 1, part, i].astype(F32)
                    sum1[m, h, part, i] = total.astype(BF16)
                    return c

                lax.fori_loop(0, SIDE, fold, 0)
                way = 1 - 2 * part
                f = first[h]
                reduce2(h, sum1.at[m, h, part, (f + 2) % SIDE], far2.at[m, h, part], way, 0)
                reduce2(h, sum1.at[m, h, part, (f + SIDE - way) % SIDE], near2.at[m, h, 1 - part, part], -way, 1 + part)
        for h in range(2):
            for d, way in ((0, 1), (1, -1)):
                got(far2.at[m, h, d], h, 1, d, 0)
                target = sum1.at[m, h, d, (first[h] + SIDE + way) % SIDE]
                target[...] = (target[...].astype(F32) + far2[m, h, d].astype(F32)).astype(BF16)
                reduce2(h, target, near2.at[m, h, d, d], way, 1 + d)
        z_copies = []
        for h in range(2):
            for part in range(2):
                for d in range(2):
                    got(near2.at[m, h, d, part], h, 1, d, 1 + part)
                total = (sum1[m, h, part, first[h]].astype(F32) + near2[m, h, 0, part].astype(F32)
                         + near2[m, h, 1, part].astype(F32))
                z_own[m, 2 * h + part] = total.astype(BF16)
                z_copies.append(send(z_own.at[m, 2 * h + part], z_got.at[m, 2 * h + part], z_send.at[2 * h + part],
                                     z_recv.at[m, 2 * h + part], z_peer))
        for q in range(4):
            z_copies[q].wait_recv()
            branch = z_own[m, q].astype(F32) + z_got[m, q].astype(F32)
            columns = pl.ds(q * quarter, quarter)
            for row in range(2):
                value = x_in[m, row, :, columns].astype(F32) + branch[8 * row:8 * row + 8] + b_down[:, columns]
                x_out[m, row, :, columns] = value.astype(BF16)

        @pl.when(phase < phases - 1)
        def _():
            next_copy(m).start()

        out[0, m] = x_out[m, z]
        for copy in sends + z_copies:
            copy.wait_send()
        return carry

    lax.fori_loop(0, micro, one, 0)

    @pl.when(phase == 0)
    def _():
        for m in range(micro):
            zx_copy(m).wait_send()

    @pl.when(phase < phases - 1)
    def _():
        for m in range(micro):
            next_copy(m).wait_send()


def on_device(phases, tokens, norm_gain, up_weight, up_bias, down_weight, down_bias):
    micro, own, depth = tokens.shape
    units = up_weight.shape[2]
    quarter = depth // 4
    vmem = pl.BlockSpec(memory_space=pltpu.VMEM)
    hbm = pl.BlockSpec(memory_space=pl.ANY)
    dma = pltpu.SemaphoreType.DMA
    return pl.pallas_call(
        functools.partial(kernel, phases),
        out_shape=jax.ShapeDtypeStruct((1, micro, own, depth), BF16),
        in_specs=[vmem, vmem, vmem, vmem, hbm, hbm],
        out_specs=vmem,
        scratch_shapes=[
            pltpu.VMEM((depth, units), BF16),
            pltpu.VMEM((units, depth), BF16),
            pltpu.VMEM((micro, 2, own, depth), BF16),
            pltpu.VMEM((micro, SIDE, SIDE, 16, depth), BF16),
            pltpu.VMEM((16 * SIDE * SIDE, units), BF16),
            pltpu.VMEM((micro, SIDE, SIDE, 16, depth), BF16),
            pltpu.VMEM((micro, 2, 2, SIDE, 16, quarter), BF16),
            pltpu.VMEM((micro, 2, 2, 2, SIDE, 16, quarter), BF16),
            pltpu.VMEM((micro, 2, 2, SIDE, 16, quarter), BF16),
            pltpu.VMEM((micro, 2, 2, 16, quarter), BF16),
            pltpu.VMEM((micro, 2, 2, 2, 16, quarter), BF16),
            pltpu.VMEM((micro, 4, 16, quarter), BF16),
            pltpu.VMEM((micro, 4, 16, quarter), BF16),
            pltpu.VMEM((micro, 2, own, depth), BF16),
            dma((2,)),
            dma((micro,)),
            dma((micro,)),
            dma((2, 2, 10)),
            dma((micro, 2, 2, 10)),
            dma((2, 2, 2, 3)),
            dma((micro, 2, 2, 2, 3)),
            dma((4,)),
            dma((micro, 4)),
            dma((micro,)),
        ],
        compiler_params=pltpu.CompilerParams(
            collective_id=0, has_side_effects=True, vmem_limit_bytes=60 * 1024 * 1024),
        name="relay",
    )(tokens, norm_gain, up_bias, down_bias, up_weight, down_weight)


def solution(mesh):
    return jax.shard_map(
        functools.partial(on_device, mesh.shape["phase"]),
        mesh=mesh,
        in_specs=(
            P(None, "blk", None),
            P("phase", None),
            P("phase", None, "blk"),
            P("phase", "blk"),
            P("phase", "blk", None),
            P("phase", None),
        ),
        out_specs=P("phase", None, "blk", None),
        check_vma=False,
    )
```

time: 1730 us -> 243 us (0.14); the launches traced: 1710 us -> 242 us
  waiting for transfers between devices: 1590 us -> 0 us
  Pallas kernels: 0 us -> 241 us
  matrix products: 78.7 us -> 0 us
    reduce_scatter x5 -> x0, waiting for transfers between devices: 822 us -> none  [on_device(): lax.psum_scatter(jnp.dot(hidden, w_down, preferred_element_type=jnp.float...]
    all_gather x5 -> x0, waiting for transfers between devices: 667 us -> none  [on_device(): lax.all_gather(normed, 'blk', axis=0, tiled=True)]
    pallas_call x0 -> x1, Pallas kernels: none -> 241 us  [on_device(): pl.pallas_call(functools.partial(kernel, phases), out_shape=jax.ShapeDtyp...]
    ppermute x4 -> x0, waiting for transfers between devices: 105 us -> none  [from_behind(): return lax.ppermute(block, axis, route)]
    dot_general x5 -> x0, matrix products: 78.7 us -> none  [on_device(): jnp.dot(hidden, w_down, preferred_element_type=jnp.float32)]
  transfers between devices with their start and end apart: 14 -> 0, of which waited for: 14 -> 0; matrix products, arithmetic and copies ran while one was open for 0% -> 0% of each run, Pallas kernels for 0% -> 0%
where the time goes in v1:
time: 243 us; the launch traced here: 242 us
  Pallas kernels  241 us (99%)
    pallas_call x1, Pallas kernels, on_device(): pl.pallas_call(functools.partial(kernel, phases), out_shape=jax.ShapeDtyp...  241 us

profile of v1, /device:TPU:65, one launch (start us, length us, event | category | flops | bytes accessed | tf_op | source)
XLA Modules:
  0.0 242.5 jit_solution(11765320971513593962)
XLA Ops:
  0.0 240.8 %relay.1 = bf16[1,2,8,6144]{3,2,1,0:T(8,128)(2,1)} custom-call(bf16[2,8,6144]{2,1,0:T(8,128)(2,1)} %tokens.1, f32[1,6144]{1,0:T(1,128)} %gain.1, f32[1,768]{1,0:T(1,128)} %b_up.1, f32[1,6144]{1,0:T(1,128)} %b_down.1, bf16[1,6144,768]{2,1,0:T(8,128)(2,1)} %w_up_hbm.1, bf16[1,768,6144]{2,1,0:T(8,128)(2,1)} %w_down_hbm.1), custom_call_target="tpu_custom_call" | custom-call | tf_op jit(solution)/shard_map/relay/pallas_call | solution.py:276
  240.8 1.6 copy.8

commit v2 on v0

v2 whole, which is shorter than its diff:
```python
import functools

import jax
import jax.numpy as jnp
from jax import lax
from jax.experimental import pallas as pl
from jax.experimental.pallas import tpu as pltpu
from jax.sharding import PartitionSpec as P

MESH = pl.DeviceIdType.MESH
SIDE = 4
ROWS = 8
F32, BF16 = jnp.float32, jnp.bfloat16
ORDER = (
    "X0", "X1", "a0", "b0", "c0", "e0", "a1", "b1", "c1", "f0", "e1", "g0", "h0", "X2", "X3", "G0",
    "f1", "g1", "a2", "h1", "b2", "c2", "U0", "a3", "e2", "D0", "E0", "f2", "G1", "b3", "g2", "U1",
    "h2", "c3", "D1", "m0", "E1", "n0", "G2", "e3", "f3", "g3", "h3", "U2", "m1", "n1", "D2", "p0",
    "r0", "E2", "G3", "U3", "p1", "r1", "D3", "m2", "E3", "q0", "s0", "n2", "m3", "q1", "s1", "n3",
    "Z0", "p2", "r2", "Z1", "p3", "r3", "q2", "s2", "q3", "s3", "Z2", "Z3",
)


def kernel(phases, tokens, gain, b_up, b_down, w_up_hbm, w_down_hbm, out,
           w_up, w_down, x_in, gathered, lhs, hidden, partial, far1, near1, sum1, near2, z_own, z_got, x_out,
           w_sem, zx_sem, in_sem, ag1_send, ag1_recv, ag2_send, ag2_recv, ag3_send, ag3_recv, rs_send, rs_recv, z_send, z_recv, next_send):
    micro, _, depth = tokens.shape
    chunks = 2 * micro
    quarter = depth // 4
    half = depth // 2
    units = w_up.shape[1]
    rows = ROWS * SIDE * SIDE
    phase = lax.axis_index("phase")
    blk = lax.axis_index("blk")
    y, z, x = blk // 8, (blk // 4) % 2, blk % 4

    def at(yy, zz, xx):
        return (phase, ((yy % SIDE) * 2 + zz) * 4 + xx % SIDE)

    def turned(odd):
        return jnp.where(odd == 1, y * 8 + (1 - z) * 4 + x, blk)

    def along(axis, t):
        return at(y, z, x + t) if axis == "x" else at(y + t, z, x)

    z_peer = at(y, 1 - z, x)
    after = ((phase + 1) % phases, turned(phase % 2))
    before = ((phase + phases - 1) % phases, turned((phase + 1) % 2))

    up_copy = pltpu.make_async_copy(w_up_hbm.at[0], w_up, w_sem.at[0])
    down_copy = pltpu.make_async_copy(w_down_hbm.at[0], w_down, w_sem.at[1])
    up_copy.start()
    down_copy.start()

    barrier = pltpu.get_barrier_semaphore()
    friends = [along(axis, t) for axis in "xy" for t in (1, 2, 3)] + [z_peer, after, before]
    for friend in friends:
        pl.semaphore_signal(barrier, inc=1, device_id=friend, device_id_type=MESH)
    pl.semaphore_wait(barrier, len(friends))

    def remote(src, dst, send_sem, recv_sem, device):
        return pltpu.make_async_remote_copy(src_ref=src, dst_ref=dst, send_sem=send_sem, recv_sem=recv_sem,
                                            device_id=device, device_id_type=MESH)

    def zx_copy(m):
        c = 2 * m + z
        return remote(tokens.at[m], x_in.at[c], zx_sem.at[m], in_sem.at[c], z_peer)

    def next_copy(c):
        return remote(x_out.at[c], x_in.at[c], next_send.at[c], in_sem.at[c], after)

    @pl.when(phase == 0)
    def _():
        for m in range(micro):
            zx_copy(m).start()
        for m in range(micro):
            x_in[2 * m + z] = tokens[m]

    sends = []

    def send(*args):
        copy = remote(*args)
        copy.start()
        sends.append(copy)

    first_axis, second_axis = ("x", "y"), ("y", "x")
    first, second = (x, y), (y, x)
    HOPS = (2, 1, 3)
    WAY = (1, 3)

    def slot(c, h, s, f):
        return gathered.at[c, s % SIDE, f % SIDE] if h == 0 else gathered.at[c, f % SIDE, s % SIDE]

    def enter(c):
        @pl.when((phase == 0) & (z != c % 2))
        def _():
            remote(tokens.at[c // 2], x_in.at[c], zx_sem.at[c // 2], in_sem.at[c], z_peer).wait_recv()

        @pl.when(phase > 0)
        def _():
            next_copy(c).wait_recv()

        wide = x_in[c].astype(F32)
        mean = jnp.mean(wide, axis=-1, keepdims=True)
        centered = wide - mean
        var = jnp.mean(centered * centered, axis=-1, keepdims=True)
        gathered[c, y, x] = (centered * lax.rsqrt(var + 1e-05) * gain[...]).astype(BF16)
        for t in HOPS:
            for h in range(2):
                block = slot(c, h, second[h], first[h]).at[:, pl.ds(h * half, half)]
                send(block, block, ag1_send.at[c, h, t - 1], ag1_recv.at[c, h, t - 1], along(first_axis[h], t))
        for h in range(2):
            relay(c, h, 0)

    def near_block(c, h, back):
        return slot(c, h, second[h], first[h] + SIDE - back).at[:, pl.ds(h * half, half)]

    def relay(c, h, back):
        block = near_block(c, h, back)
        for d in range(2):
            send(block, block, ag2_send.at[c, h, d, back], ag2_recv.at[c, h, d, back], along(second_axis[h], WAY[d]))

    def pass_on(c, back):
        for h in range(2):
            block = slot(c, h, 0, 0).at[:, pl.ds(0, half)]
            remote(block, block, ag1_send.at[c, h, back - 1], ag1_recv.at[c, h, back - 1], z_peer).wait_recv()
            relay(c, h, back)

    def forward(c, back):
        for d in range(2):
            for h in range(2):
                block = slot(c, h, 0, 0).at[:, pl.ds(0, half)]
                remote(block, block, ag2_send.at[c, h, d, back], ag2_recv.at[c, h, d, back], z_peer).wait_recv()
                block = slot(c, h, second[h] + SIDE - WAY[d], first[h] + SIDE - back).at[:, pl.ds(h * half + d * quarter, quarter)]
                send(block, block, ag3_send.at[c, h, d, back], ag3_recv.at[c, h, d, back], along(second_axis[h], WAY[d]))

    def collect(c):
        for back in range(SIDE):
            for d in range(2):
                for h in range(2):
                    block = slot(c, h, 0, 0).at[:, pl.ds(0, quarter)]
                    remote(block, block, ag3_send.at[c, h, d, back], ag3_recv.at[c, h, d, back], z_peer).wait_recv()

        def pack(i, carry):
            yy, xx = i // 2, (i % 2) * 2
            pair = jnp.concatenate([gathered[c, yy, xx].astype(F32), gathered[c, yy, xx + 1].astype(F32)], axis=0)
            lhs[pl.ds(pl.multiple_of(i * 2 * ROWS, 2 * ROWS), 2 * ROWS), :] = pair.astype(BF16)
            return carry

        lax.fori_loop(0, rows // (2 * ROWS), pack, 0)

    def up(c):
        if c == 0:
            up_copy.wait()
        wide_n = min(256, units)

        def tile(n, carry):
            columns = pl.ds(pl.multiple_of(n * wide_n, wide_n), wide_n)
            value = jnp.dot(lhs[...], w_up[:, columns], preferred_element_type=F32) + b_up[:, columns]
            hidden[:, columns] = jax.nn.gelu(value).astype(BF16)
            return carry

        lax.fori_loop(0, units // wide_n, tile, 0)

    def strip(c, h, part, s):
        return partial.at[c, h, part, s % SIDE]

    def reduce_send(c, h, stage, src, dst, d, index):
        send(src, dst, rs_send.at[c, h, stage, d, index], rs_recv.at[c, h, stage, d, index],
             along(second_axis[h], WAY[d]))

    def got(c, h, stage, d, index, ref):
        remote(ref, ref, rs_send.at[c, h, stage, d, index], rs_recv.at[c, h, stage, d, index], z_peer).wait_recv()

    def down(c, part):
        if c == 0 and part == 0:
            down_copy.wait()
        wide_q = min(512, quarter)
        for h in range(2):
            base = h * half + part * quarter

            def tile(n, carry):
                start = pl.multiple_of(n * wide_q, wide_q)
                value = jnp.dot(hidden[...], w_down[:, pl.ds(base + start, wide_q)], preferred_element_type=F32)
                value = value.reshape(SIDE, SIDE, ROWS, wide_q).astype(BF16)
                for i in range(SIDE):
                    if h == 0:
                        partial[c, h, part, i, :, :, pl.ds(start, wide_q)] = value[i]
                    else:
                        partial[c, h, part, :, i, :, pl.ds(start, wide_q)] = value[i]
                return carry

            lax.fori_loop(0, quarter // wide_q, tile, 0)
            reduce_send(c, h, 0, strip(c, h, part, second[h] + 2), far1.at[c, h, part], part, 0)
            reduce_send(c, h, 0, strip(c, h, part, second[h] + WAY[1 - part]), near1.at[c, h, 1 - part, part],
                        1 - part, 1 + part)

    def merge(c, part):
        for h in range(2):
            got(c, h, 0, part, 0, far1.at[c, h, part])
            target = strip(c, h, part, second[h] + WAY[part])

            def fold(i, carry):
                target[i] = (target[i].astype(F32) + far1[c, h, part, i].astype(F32)).astype(BF16)
                return carry

            lax.fori_loop(0, SIDE, fold, 0)
            reduce_send(c, h, 0, target, near1.at[c, h, part, part], part, 1 + part)

    def reduce1(c, part):
        for h in range(2):
            for d in range(2):
                got(c, h, 0, d, 1 + part, near1.at[c, h, d, part])
            mine = strip(c, h, part, second[h])

            def fold(i, carry):
                total = mine[i].astype(F32)
                for d in range(2):
                    total = total + near1[c, h, d, part, i].astype(F32)
                sum1[c, h, part, i] = total.astype(BF16)
                return carry

            lax.fori_loop(0, SIDE, fold, 0)
            for t in HOPS:
                send(sum1.at[c, h, part, (first[h] + t) % SIDE], near2.at[c, h, t - 1, part],
                     rs_send.at[c, h, 1, t - 1, part], rs_recv.at[c, h, 1, t - 1, part], along(first_axis[h], t))

    def z_copy(c, h, part):
        return remote(z_own.at[c, h, part], z_got.at[c, h, part], z_send.at[c, h, part], z_recv.at[c, h, part], z_peer)

    def reduce2(c, part):
        if True:
            for h in range(2):
                for t in HOPS:
                    ref = near2.at[c, h, t - 1, part]
                    remote(ref, ref, rs_send.at[c, h, 1, t - 1, part], rs_recv.at[c, h, 1, t - 1, part], z_peer).wait_recv()
                total = sum1[c, h, part, first[h]].astype(F32)
                for t in range(3):
                    total = total + near2[c, h, t, part].astype(F32)
                z_own[c, h, part] = total.astype(BF16)
                copy = z_copy(c, h, part)
                copy.start()
                sends.append(copy)

    def leave(c):
        for part in range(2):
            for h in range(2):
                z_copy(c, h, part).wait_recv()
                branch = z_own[c, h, part].astype(F32) + z_got[c, h, part].astype(F32)
                columns = pl.ds(h * half + part * quarter, quarter)
                x_out[c, :, columns] = (x_in[c, :, columns].astype(F32) + branch + b_down[:, columns]).astype(BF16)

        @pl.when(phase < phases - 1)
        def _():
            next_copy(c).start()

        @pl.when(z == c % 2)
        def _():
            out[0, c // 2] = x_out[c]

    steps = {"X": (enter,), "a": (pass_on, 1), "b": (pass_on, 3), "c": (pass_on, 2), "G": (collect,), "U": (up,), "D": (down, 0), "E": (down, 1),
             "e": (forward, 0), "f": (forward, 1), "g": (forward, 3), "h": (forward, 2), "m": (merge, 0), "n": (merge, 1),
             "p": (reduce1, 0), "r": (reduce1, 1), "q": (reduce2, 0), "s": (reduce2, 1), "Z": (leave,)}
    for step in ORDER:
        fn, *more = steps[step[0]]
        fn(int(step[1]), *more)

    for copy in sends:
        copy.wait_send()

    @pl.when(phase == 0)
    def _():
        for m in range(micro):
            zx_copy(m).wait_send()

    @pl.when(phase < phases - 1)
    def _():
        for c in range(chunks):
            next_copy(c).wait_send()


def on_device(phases, tokens, norm_gain, up_weight, up_bias, down_weight, down_bias):
    micro, own, depth = tokens.shape
    units = up_weight.shape[2]
    quarter = depth // 4
    chunks = 2 * micro
    vmem = pl.BlockSpec(memory_space=pltpu.VMEM)
    hbm = pl.BlockSpec(memory_space=pl.ANY)
    dma = pltpu.SemaphoreType.DMA
    return pl.pallas_call(
        functools.partial(kernel, phases),
        out_shape=jax.ShapeDtypeStruct((1, micro, own, depth), BF16),
        in_specs=[vmem, vmem, vmem, vmem, hbm, hbm],
        out_specs=vmem,
        scratch_shapes=[
            pltpu.VMEM((depth, units), BF16),
            pltpu.VMEM((units, depth), BF16),
            pltpu.VMEM((chunks, ROWS, depth), BF16),
            pltpu.VMEM((chunks, SIDE, SIDE, ROWS, depth), BF16),
            pltpu.VMEM((ROWS * SIDE * SIDE, depth), BF16),
            pltpu.VMEM((ROWS * SIDE * SIDE, units), BF16),
            pltpu.VMEM((chunks, 2, 2, SIDE, SIDE, ROWS, quarter), BF16),
            pltpu.VMEM((chunks, 2, 2, SIDE, ROWS, quarter), BF16),
            pltpu.VMEM((chunks, 2, 2, 2, SIDE, ROWS, quarter), BF16),
            pltpu.VMEM((chunks, 2, 2, SIDE, ROWS, quarter), BF16),
            pltpu.VMEM((chunks, 2, 3, 2, ROWS, quarter), BF16),
            pltpu.VMEM((chunks, 2, 2, ROWS, quarter), BF16),
            pltpu.VMEM((chunks, 2, 2, ROWS, quarter), BF16),
            pltpu.VMEM((chunks, ROWS, depth), BF16),
            dma((2,)),
            dma((micro,)),
            dma((chunks,)),
            dma((chunks, 2, 3)),
            dma((chunks, 2, 3)),
            dma((chunks, 2, 2, 4)),
            dma((chunks, 2, 2, 4)),
            dma((chunks, 2, 2, 4)),
            dma((chunks, 2, 2, 4)),
            dma((chunks, 2, 2, 3, 3)),
            dma((chunks, 2, 2, 3, 3)),
            dma((chunks, 2, 2)),
            dma((chunks, 2, 2)),
            dma((chunks,)),
        ],
        compiler_params=pltpu.CompilerParams(
            collective_id=0, has_side_effects=True, vmem_limit_bytes=60 * 1024 * 1024),
        name="relay",
    )(tokens, norm_gain, up_bias, down_bias, up_weight, down_weight)


def solution(mesh):
    return jax.shard_map(
        functools.partial(on_device, mesh.shape["phase"]),
        mesh=mesh,
        in_specs=(
            P(None, "blk", None),
            P("phase", None),
            P("phase", None, "blk"),
            P("phase", "blk"),
            P("phase", "blk", None),
            P("phase", None),
        ),
        out_specs=P("phase", None, "blk", None),
        check_vma=False,
    )
```

time: 1730 us -> 194 us (0.11); the launches traced: 1710 us -> 194 us
  waiting for transfers between devices: 1590 us -> 0 us
  Pallas kernels: 0 us -> 193 us
  matrix products: 78.7 us -> 0 us
    reduce_scatter x5 -> x0, waiting for transfers between devices: 822 us -> none  [on_device(): lax.psum_scatter(jnp.dot(hidden, w_down, preferred_element_type=jnp.float...]
    all_gather x5 -> x0, waiting for transfers between devices: 667 us -> none  [on_device(): lax.all_gather(normed, 'blk', axis=0, tiled=True)]
    pallas_call x0 -> x1, Pallas kernels: none -> 193 us  [on_device(): pl.pallas_call(functools.partial(kernel, phases), out_shape=jax.ShapeDtyp...]
    ppermute x4 -> x0, waiting for transfers between devices: 105 us -> none  [from_behind(): return lax.ppermute(block, axis, route)]
    dot_general x5 -> x0, matrix products: 78.7 us -> none  [on_device(): jnp.dot(hidden, w_down, preferred_element_type=jnp.float32)]
  transfers between devices with their start and end apart: 14 -> 0, of which waited for: 14 -> 0; matrix products, arithmetic and copies ran while one was open for 0% -> 0% of each run, Pallas kernels for 0% -> 0%
where the time goes in v2:
time: 194 us
  Pallas kernels  193 us (99%)
    pallas_call x1, Pallas kernels, on_device(): pl.pallas_call(functools.partial(kernel, phases), out_shape=jax.ShapeDtyp...  193 us

profile of v2, /device:TPU:65, one launch (start us, length us, event | category | flops | bytes accessed | tf_op | source)
XLA Modules:
  0.0 194.4 jit_solution(11501972391919421806)
XLA Ops:
  0.0 192.7 %relay.1 = bf16[1,2,8,6144]{3,2,1,0:T(8,128)(2,1)} custom-call(bf16[2,8,6144]{2,1,0:T(8,128)(2,1)} %tokens.1, f32[1,6144]{1,0:T(1,128)} %gain.1, f32[1,768]{1,0:T(1,128)} %b_up.1, f32[1,6144]{1,0:T(1,128)} %b_down.1, bf16[1,6144,768]{2,1,0:T(8,128)(2,1)} %w_up_hbm.1, bf16[1,768,6144]{2,1,0:T(8,128)(2,1)} %w_down_hbm.1), custom_call_target="tpu_custom_call" | custom-call | tf_op jit(solution)/shard_map/relay/pallas_call | solution.py:289
  192.7 1.6 copy.8

commit v3 on v2

--- a/solution.py
+++ b/solution.py
@@ -12,11 +12,11 @@
 ROWS = 8
 F32, BF16 = jnp.float32, jnp.bfloat16
 ORDER = (
-    "X0", "X1", "a0", "b0", "c0", "e0", "a1", "b1", "c1", "f0", "e1", "g0", "h0", "X2", "X3", "G0",
-    "f1", "g1", "a2", "h1", "b2", "c2", "U0", "a3", "e2", "D0", "E0", "f2", "G1", "b3", "g2", "U1",
-    "h2", "c3", "D1", "m0", "E1", "n0", "G2", "e3", "f3", "g3", "h3", "U2", "m1", "n1", "D2", "p0",
-    "r0", "E2", "G3", "U3", "p1", "r1", "D3", "m2", "E3", "q0", "s0", "n2", "m3", "q1", "s1", "n3",
-    "Z0", "p2", "r2", "Z1", "p3", "r3", "q2", "s2", "q3", "s3", "Z2", "Z3",
+    "X0", "X1", "a0", "b0", "c0", "e0", "a1", "X2", "f0", "g0", "h0", "b1", "c1", "e1", "a2", "b2",
+    "c2", "X3", "G0", "f1", "U0", "g1", "h1", "e2", "D0", "a3", "b3", "c3", "f2", "g2", "h2", "E0",
+    "G1", "U1", "e3", "D1", "f3", "m0", "g3", "h3", "E1", "G2", "U2", "n0", "m1", "D2", "E2", "G3",
+    "n1", "U3", "p1", "p0", "r0", "D3", "m2", "r1", "n2", "E3", "q0", "s0", "q1", "m3", "p2", "s1",
+    "r2", "Z0", "n3", "Z1", "q2", "p3", "s2", "r3", "Z2", "q3", "s3", "Z3",
 )
 
 

time: 194 us -> 192 us (0.990)
  Pallas kernels: 193 us -> 190 us
    pallas_call x1, Pallas kernels: 193 us -> 190 us  [on_device(): pl.pallas_call(functools.partial(kernel, phases), out_shape=jax.ShapeDtyp...]
where the time goes in v3:
time: 192 us
  Pallas kernels  190 us (99%)
    pallas_call x1, Pallas kernels, on_device(): pl.pallas_call(functools.partial(kernel, phases), out_shape=jax.ShapeDtyp...  190 us

profile of v3, /device:TPU:65, one launch (start us, length us, event | category | flops | bytes accessed | tf_op | source)
XLA Modules:
  0.0 191.9 jit_solution(4136467244480288487)
XLA Ops:
  0.0 190.3 %relay.1 = bf16[1,2,8,6144]{3,2,1,0:T(8,128)(2,1)} custom-call(bf16[2,8,6144]{2,1,0:T(8,128)(2,1)} %tokens.1, f32[1,6144]{1,0:T(1,128)} %gain.1, f32[1,768]{1,0:T(1,128)} %b_up.1, f32[1,6144]{1,0:T(1,128)} %b_down.1, bf16[1,6144,768]{2,1,0:T(8,128)(2,1)} %w_up_hbm.1, bf16[1,768,6144]{2,1,0:T(8,128)(2,1)} %w_down_hbm.1), custom_call_target="tpu_custom_call" | custom-call | tf_op jit(solution)/shard_map/relay/pallas_call | solution.py:289
  190.3 1.6 copy.8

commit v4 on v3

--- a/solution.py
+++ b/solution.py
@@ -22,7 +22,7 @@
 
 def kernel(phases, tokens, gain, b_up, b_down, w_up_hbm, w_down_hbm, out,
            w_up, w_down, x_in, gathered, lhs, hidden, partial, far1, near1, sum1, near2, z_own, z_got, x_out,
-           w_sem, zx_sem, in_sem, ag1_send, ag1_recv, ag2_send, ag2_recv, ag3_send, ag3_recv, rs_send, rs_recv, z_send, z_recv, next_send):
+           w_sem, zx_sem, in_sem, ag1_send, ag1_recv, ag2_send, ag2_recv, ag3_send, ag3_recv, rs_send, rs_recv, z_send, z_recv, next_send, next_recv):
     micro, _, depth = tokens.shape
     chunks = 2 * micro
     quarter = depth // 4
@@ -65,8 +65,9 @@
         c = 2 * m + z
         return remote(tokens.at[m], x_in.at[c], zx_sem.at[m], in_sem.at[c], z_peer)
 
-    def next_copy(c):
-        return remote(x_out.at[c], x_in.at[c], next_send.at[c], in_sem.at[c], after)
+    def next_copy(c, q):
+        cut = pl.ds(q * quarter, quarter)
+        return remote(x_out.at[c, :, cut], x_in.at[c, :, cut], next_send.at[c, q], next_recv.at[c, q], after)
 
     @pl.when(phase == 0)
     def _():
@@ -97,7 +98,8 @@
 
         @pl.when(phase > 0)
         def _():
-            next_copy(c).wait_recv()
+            for q in range(4):
+                next_copy(c, q).wait_recv()
 
         wide = x_in[c].astype(F32)
         mean = jnp.mean(wide, axis=-1, keepdims=True)
@@ -249,9 +251,9 @@
                 columns = pl.ds(h * half + part * quarter, quarter)
                 x_out[c, :, columns] = (x_in[c, :, columns].astype(F32) + branch + b_down[:, columns]).astype(BF16)
 
-        @pl.when(phase < phases - 1)
-        def _():
-            next_copy(c).start()
+                @pl.when(phase < phases - 1)
+                def _():
+                    next_copy(c, 2 * h + part).start()
 
         @pl.when(z == c % 2)
         def _():
@@ -275,7 +277,8 @@
     @pl.when(phase < phases - 1)
     def _():
         for c in range(chunks):
-            next_copy(c).wait_send()
+            for q in range(4):
+                next_copy(c, q).wait_send()
 
 
 def on_device(phases, tokens, norm_gain, up_weight, up_bias, down_weight, down_bias):
@@ -319,7 +322,8 @@
             dma((chunks, 2, 2, 3, 3)),
             dma((chunks, 2, 2)),
             dma((chunks, 2, 2)),
-            dma((chunks,)),
+            dma((chunks, 4)),
+            dma((chunks, 4)),
         ],
         compiler_params=pltpu.CompilerParams(
             collective_id=0, has_side_effects=True, vmem_limit_bytes=60 * 1024 * 1024),

time: 192 us -> 192 us (level)
  no operation moved by 1% of the time
where the time goes in v4:
time: 192 us
  Pallas kernels  191 us (99%)
    pallas_call x1, Pallas kernels, on_device(): pl.pallas_call(functools.partial(kernel, phases), out_shape=jax.ShapeDtyp...  191 us

profile of v4, /device:TPU:65, one launch (start us, length us, event | category | flops | bytes accessed | tf_op | source)
XLA Modules:
  0.0 192.3 jit_solution(15154583343373891461)
XLA Ops:
  0.0 190.7 %relay.1 = bf16[1,2,8,6144]{3,2,1,0:T(8,128)(2,1)} custom-call(bf16[2,8,6144]{2,1,0:T(8,128)(2,1)} %tokens.1, f32[1,6144]{1,0:T(1,128)} %gain.1, f32[1,768]{1,0:T(1,128)} %b_up.1, f32[1,6144]{1,0:T(1,128)} %b_down.1, bf16[1,6144,768]{2,1,0:T(8,128)(2,1)} %w_up_hbm.1, bf16[1,768,6144]{2,1,0:T(8,128)(2,1)} %w_down_hbm.1), custom_call_target="tpu_custom_call" | custom-call | tf_op jit(solution)/shard_map/relay/pallas_call | solution.py:292
  190.7 1.6 copy.8
